TPU v7x, 32 devices: a whole 2x2x4 slice. The times are simulated.
32 devices in a mesh: group: 2 (over y), seq: 4 (over z), fsdp: 4 (over x, core).
Axes of the slice: x: 2, y: 2, z: 4, core: 2. Of those that a mesh axis runs over, the one named last changes fastest.
Arguments:
- tile_patches: bfloat16 [64, 256, 1536], P(('group', 'seq', 'fsdp')), parts along dimension 0, may hold values from -6 to 6
- vit_gain: float32 [1536], replicated, may hold values from 0.25 to 1.75
- w_query: bfloat16 [1536, 768], P('fsdp'), may hold values from -0.15625 to 0.15625
- w_key: bfloat16 [1536, 768], P('fsdp'), may hold values from -0.15625 to 0.15625
- w_value: bfloat16 [1536, 768], P('fsdp'), may hold values from -0.15625 to 0.15625
- w_out: bfloat16 [768, 1536], P('fsdp'), may hold values from -0.21875 to 0.21875
- w_proj: bfloat16 [1536, 768], P('fsdp'), may hold values from -0.15625 to 0.15625
- long_gain: float32 [768], replicated, may hold values from 0.25 to 1.75
- long_query: bfloat16 [768, 768], P(None, 'fsdp'), may hold values from -0.21875 to 0.21875
- long_key: bfloat16 [768, 768], P(None, 'fsdp'), may hold values from -0.21875 to 0.21875
- long_value: bfloat16 [768, 768], P(None, 'fsdp'), may hold values from -0.21875 to 0.21875
- long_out: bfloat16 [768, 768], P('fsdp'), may hold values from -0.21875 to 0.21875
- seq_order: int32 [64], P(('group', 'seq', 'fsdp')), parts along dimension 0, may hold values from 0 to 31, each once
- counts: int32 [32], P(('group', 'seq', 'fsdp')), parts along dimension 0, may hold values from 1 to 2
Outputs:
- encoded: bfloat16 [64, 768], P(('group', 'seq'), 'fsdp'), parts along dimension 0
There are 2 independent parts, one for each index of `group`. A program takes and returns all parts, laid end to end along the dimension named above; an argument that names none is the same for every part. Nothing has to cross between parts.
Inputs may be any that keep to these rules, and one draw needn't show every extreme that they name: `seq_order`: each of the 32 sequence positions belongs to exactly one tile. In each block of 2 consecutive tiles the first counts tiles are tissue.
All inputs are finite; a program needn't handle non-finite values.
Results may differ from a plain program's by a relative error of at most 0.013.
Values may be sent and summed in bfloat16 or wider, within the bound.
No kernel may reach another device: no remote copies, remote signals or barrier semaphores. Data moves between devices by JAX's collectives and lax.ppermute only.
A program may use at most 64 MiB of HBM per device.

v0:
```python
import math
import jax
import jax.numpy as jnp
from jax import lax
from jax.sharding import PartitionSpec as P

VHD = 64
HEADS = 16
DILATION_STEP = 4
EPSILON = 1e-06


def layer_norm(inputs, norm_gain):
    widened = inputs.astype(jnp.float32)
    average = jnp.mean(widened, axis=-1, keepdims=True)
    centred = widened - average
    variance = jnp.mean(centred * centred, axis=-1, keepdims=True)
    return (centred * lax.rsqrt(variance + EPSILON) * norm_gain).astype(jnp.bfloat16)


def dilated_attention(
    query_rows,
    key_rows,
    value_rows,
    query_position_index,
    key_position_index,
    key_present,
    leading_head,
    head_total_count,
    segment,
):
    head_size = query_rows.shape[1] // head_total_count
    query_heads = query_rows.reshape(query_rows.shape[0], head_total_count, head_size)
    key_heads = key_rows.reshape(key_rows.shape[0], head_total_count, head_size)
    value_heads = value_rows.reshape(value_rows.shape[0], head_total_count, head_size)
    scores = jnp.einsum(
        "rhd,khd->hrk", query_heads, key_heads, preferred_element_type=jnp.float32
    ) / math.sqrt(head_size)
    itself = query_position_index[:, None] == key_position_index[None, :]
    permitted_mask = (key_present[None, :] > 0) | itself
    in_local = (
        query_position_index[:, None] // segment == key_position_index[None, :] // segment
    ) & permitted_mask
    head_shift_amounts = (
        leading_head + jnp.arange(head_total_count, dtype=jnp.int32)
    ) % DILATION_STEP
    within_dilated_set = (
        ((query_position_index % DILATION_STEP)[None, :, None] == head_shift_amounts[:, None, None])
        & ((key_position_index % DILATION_STEP)[None, None, :] == head_shift_amounts[:, None, None])
        & permitted_mask[None]
    )
    lifted = jnp.exp(scores)
    local_weights = jnp.where(in_local[None], lifted, 0.0)
    dilated_weights = jnp.where(within_dilated_set, lifted, 0.0)
    denominator = jnp.sum(local_weights, axis=-1) + jnp.sum(dilated_weights, axis=-1)
    numerator = jnp.einsum(
        "hrk,khd->rhd",
        local_weights.astype(jnp.bfloat16),
        value_heads,
        preferred_element_type=jnp.float32,
    )
    numerator = numerator + jnp.einsum(
        "hrk,khd->rhd",
        dilated_weights.astype(jnp.bfloat16),
        value_heads,
        preferred_element_type=jnp.float32,
    )
    combined = numerator / jnp.transpose(denominator)[:, :, None]
    return combined.reshape(query_rows.shape[0], head_total_count * head_size).astype(jnp.bfloat16)


def local(
    tile_patches,
    vit_gain,
    w_query,
    w_key,
    w_value,
    w_out,
    w_proj,
    long_gain,
    long_query,
    long_key,
    long_value,
    long_out,
    seq_order,
    counts,
):
    seq_size = lax.axis_size("seq")
    group_size = lax.axis_size("fsdp")
    tile_count, patch_count, width = tile_patches.shape
    normed = layer_norm(tile_patches, vit_gain)
    class_normed = normed[:, 0, :]
    vit_width = w_key.shape[1]
    vit_heads = vit_width // VHD
    full_query, full_out, full_proj = (
        lax.all_gather(w_query, "fsdp", axis=0, tiled=True),
        lax.all_gather(w_out, "fsdp", axis=0, tiled=True),
        lax.all_gather(w_proj, "fsdp", axis=0, tiled=True),
    )
    query_row = jnp.dot(class_normed, full_query, preferred_element_type=jnp.float32).astype(
        jnp.bfloat16
    )
    group_query = lax.all_gather(query_row, "fsdp", axis=0, tiled=True)
    rows_local = w_key.shape[0]
    key_heads_local = w_key.reshape(rows_local, vit_heads, VHD)
    query_group = group_query.reshape(group_query.shape[0], vit_heads, VHD)
    key_part = jnp.einsum(
        "ihd,thd->thi", key_heads_local, query_group, preferred_element_type=jnp.float32
    )
    folded = lax.all_to_all(
        key_part.astype(jnp.bfloat16), "fsdp", split_axis=0, concat_axis=2, tiled=True
    ).astype(key_part.dtype)
    scores = jnp.einsum(
        "tpi,thi->thp", normed.astype(jnp.float32), folded, precision=lax.Precision.HIGHEST
    ) / math.sqrt(VHD)
    lifted = jnp.exp(scores)
    attn_probs = (lifted / jnp.sum(lifted, axis=-1, keepdims=True)).astype(jnp.bfloat16)
    mixed = jnp.einsum("thp,tpi->thi", attn_probs, normed, preferred_element_type=jnp.float32)
    spread_rows = lax.all_to_all(
        mixed.astype(jnp.bfloat16), "fsdp", split_axis=2, concat_axis=0, tiled=True
    ).astype(mixed.dtype)
    value_heads_local = w_value.reshape(rows_local, vit_heads, VHD).astype(jnp.float32)
    summed_heads = jnp.einsum(
        "thi,ihd->thd", spread_rows, value_heads_local, precision=lax.Precision.HIGHEST
    )
    pooled = lax.psum_scatter(
        summed_heads.reshape(tile_count * lax.axis_size("fsdp"), vit_width).astype(jnp.bfloat16),
        "fsdp",
        scatter_dimension=0,
        tiled=True,
    ).astype(jnp.float32)
    pooled = pooled.astype(jnp.bfloat16)
    class_input = tile_patches[:, 0, :].astype(jnp.float32)
    class_row = (
        class_input + jnp.dot(pooled, full_out, preferred_element_type=jnp.float32)
    ).astype(jnp.bfloat16)
    embeds = jnp.dot(class_row, full_proj, preferred_element_type=jnp.float32).astype(jnp.bfloat16)
    tile_slot = jnp.arange(tile_count, dtype=jnp.int32)
    present = (tile_slot < counts[0]).astype(jnp.int32)
    embeds = jnp.where(present[:, None] > 0, embeds, jnp.zeros_like(embeds))
    model_width = embeds.shape[1]
    rows_dev = tile_count * group_size
    total_tiles = rows_dev * seq_size
    segment = total_tiles // 4
    head_width = long_query.shape[1]
    heads_dev = head_width // (model_width // HEADS)
    leading_head = lax.axis_index("fsdp") * heads_dev
    targets = lax.axis_index("seq") * rows_dev + jnp.arange(rows_dev, dtype=jnp.int32)
    column_start = lax.axis_index("fsdp") * head_width
    all_embeds, all_order, all_present = (
        lax.all_gather(embeds, ("seq", "fsdp"), axis=0, tiled=True),
        lax.all_gather(seq_order, ("seq", "fsdp"), axis=0, tiled=True),
        lax.all_gather(present, ("seq", "fsdp"), axis=0, tiled=True),
    )
    picker = all_order[None, :] == targets[:, None]
    mine = jnp.dot(
        picker.astype(jnp.bfloat16), all_embeds, preferred_element_type=jnp.float32
    ).astype(jnp.bfloat16)
    mine_present = jnp.sum(jnp.where(picker, all_present[None, :], 0), axis=1).astype(jnp.int32)
    long_normed = layer_norm(mine, long_gain)
    query_rows = jnp.dot(long_normed, long_query, preferred_element_type=jnp.float32).astype(
        jnp.bfloat16
    )
    key_local = jnp.dot(long_normed, long_key, preferred_element_type=jnp.float32).astype(
        jnp.bfloat16
    )
    value_local = jnp.dot(long_normed, long_value, preferred_element_type=jnp.float32).astype(
        jnp.bfloat16
    )
    key_rows, value_rows, key_present = (
        lax.all_gather(key_local, "seq", axis=0, tiled=True),
        lax.all_gather(value_local, "seq", axis=0, tiled=True),
        lax.all_gather(mine_present, "seq", axis=0, tiled=True),
    )
    key_position_index = jnp.arange(total_tiles, dtype=jnp.int32)
    residual = lax.dynamic_slice_in_dim(mine, column_start, head_width, 1)
    attended = dilated_attention(
        query_rows,
        key_rows,
        value_rows,
        targets,
        key_position_index,
        key_present,
        leading_head,
        heads_dev,
        segment,
    )
    head_terms = jnp.dot(attended, long_out, preferred_element_type=jnp.float32)
    summed = lax.psum_scatter(
        head_terms.astype(jnp.bfloat16), "fsdp", scatter_dimension=1, tiled=True
    ).astype(jnp.float32)
    return (residual.astype(jnp.float32) + summed).astype(jnp.bfloat16)


def solution(mesh):
    return jax.shard_map(
        local,
        mesh=mesh,
        in_specs=(
            P(("group", "seq", "fsdp"), None, None),
            P(),
            P("fsdp", None),
            P("fsdp", None),
            P("fsdp", None),
            P("fsdp", None),
            P("fsdp", None),
            P(),
            P(None, "fsdp"),
            P(None, "fsdp"),
            P(None, "fsdp"),
            P("fsdp", None),
            P(("group", "seq", "fsdp")),
            P(("group", "seq", "fsdp")),
        ),
        out_specs=P(("group", "seq"), "fsdp"),
        check_vma=False,
    )
```

profile of v0, /device:TPU:0, one launch (start us, length us, event | category | flops | bytes accessed | tf_op | source)
XLA Modules:
  0.0 166.9 jit_solution(15862712524347487263)
XLA Ops:
  6.5 0.7 all-gather.6.cloned.1.call-update
  7.3 0.0 all-gather.10.cloned.1.call-start
  7.3 0.7 all-gather.10.cloned.1.call-update
  8.0 0.0 all-gather.8.cloned.1.call-start
  8.1 0.7 all-gather.8.cloned.1.call-update
  8.8 0.3 convert_reduce_fusion
  9.1 0.5 fusion.2
  10.3 0.5 fusion.4
  10.9 0.6 dynamic-slice
  12.1 0.1 fusion.55
  12.3 2.1 %copy.37 = bf16[384,768]{0,1:T(8,128)(2,1)} copy(bf16[384,768]{1,0:T(8,128)(2,1)} %param.17) | data formatting | bytes 1179648 | tf_op args[3]
  14.4 0.6 dynamic-slice.2
  15.0 0.2 dynamic-update-slice
  15.8 13.8 %all-reduce.4 = (s32[32]{0:T(128)S(1)}, s32[32]{0:T(128)S(1)}) all-reduce(s32[32]{0:T(128)S(1)} %dynamic-update-slice, s32[32]{0:T(128)S(1)} %fusion.55), channel_id=1, replica_groups=mesh['group'=2,'seq'=4,'fsdp'=4] {'seq','fsdp'}, use_global_device_ids=true, to_apply=%add | all-reduce | flops 64 | bytes 512
  29.6 0.2 fusion.46
  29.8 0.2 dynamic-update-slice.2
  30.0 6.2 %all-reduce.2 = s32[32]{0:T(128)S(1)} all-reduce(s32[32]{0:T(128)S(1)} %dynamic-update-slice.2), channel_id=1, replica_groups=mesh['group'=2,'seq'=4,'fsdp'=4] {'seq'}, use_global_device_ids=true, to_apply=%add.2 | all-reduce | flops 32 | bytes 256
  36.3 0.1 broadcast_compare_fusion.1
  36.4 0.1 fusion.47
  36.5 2.1 %fusion.17 = bf16[1,2,768]{2,1,0:T(2,128)(2,1)S(1)} fusion(bf16[1536,768]{1,0:T(8,128)(2,1)} %all-gather.6.cloned.1.call-done, bf16[2,1,1536]{2,1,0:T(2,128)(2,1)S(1)} %slice.8), kind=kOutput, calls=%fused_computation.32 | convolution fusion | flops 4720128 | bytes 2368512 | tf_op jit(solution)/shard_map/dot_general | solution.py:100
  38.6 5.2 %all-gather = bf16[4,2,768]{2,1,0:T(2,128)(2,1)S(1)} all-gather(bf16[1,2,768]{2,1,0:T(2,128)(2,1)S(1)} %fusion.17), channel_id=1, replica_groups=mesh['group'=2,'seq'=4,'fsdp'=4] {'fsdp'}, dimensions={0}, use_global_device_ids=true | all-gather | bytes 15360 | tf_op jit(solution)/shard_map/all_gather | solution.py:103
  43.8 0.1 reshape.332
  43.9 0.2 fusion.6
  44.1 0.7 copy.39
  44.8 3.3 %all-to-all-start = ((bf16[8,12,384]{2,1,0:T(8,128)(2,1)}), bf16[8,12,384]{2,1,0:T(8,128)(2,1)S(1)}, u32[]{:S(2)}, u32[]{:S(2)}) async-start(bf16[8,12,384]{2,1,0:T(8,128)(2,1)} %copy.39), calls=%async_computation | async-start | bytes 196608 | tf_op jit(solution)/shard_map/all_to_all | solution.py:110
  48.1 0.1 broadcast_compare_fusion
  48.2 5.6 %all-to-all-done = bf16[8,12,384]{2,1,0:T(8,128)(2,1)S(1)} async-done(((bf16[8,12,384]{2,1,0:T(8,128)(2,1)}), bf16[8,12,384]{2,1,0:T(8,128)(2,1)S(1)}, u32[]{:S(2)}, u32[]{:S(2)}) %all-to-all-start) | async-done | bytes 73760 | tf_op jit(solution)/shard_map/all_to_all | solution.py:110
  53.9 0.5 fusion.7
  54.4 0.4 convolution_convert_fusion
  54.8 0.6 copy.42
  55.4 2.1 %reshape.362 = bf16[4,2,4608]{2,1,0:T(2,128)(2,1)} reshape(bf16[1536,2,12]{2,1,0:T(2,128)(2,1)S(1)} %bitcast.61) | data formatting | bytes 147456
  57.5 3.3 %all-to-all-start.1 = ((bf16[4,2,4608]{2,1,0:T(2,128)(2,1)}), bf16[4,2,4608]{2,1,0:T(2,128)(2,1)S(1)}, u32[]{:S(2)}, u32[]{:S(2)}) async-start(bf16[4,2,4608]{2,1,0:T(2,128)(2,1)} %reshape.362), calls=%async_computation.1 | async-start | bytes 147456 | tf_op jit(solution)/shard_map/all_to_all | solution.py:119
  60.8 0.0 reduce-scatter.4.cloned.1.call-start
  60.9 0.3 copy.45
  61.2 0.6 dynamic-slice.3
  62.5 2.5 %all-to-all-done.1 = bf16[4,2,4608]{2,1,0:T(2,128)(2,1)S(1)} async-done(((bf16[4,2,4608]{2,1,0:T(2,128)(2,1)}), bf16[4,2,4608]{2,1,0:T(2,128)(2,1)S(1)}, u32[]{:S(2)}, u32[]{:S(2)}) %all-to-all-start.1) | async-done | bytes 73760 | tf_op jit(solution)/shard_map/all_to_all | solution.py:119
  65.0 1.8 %reshape.363 = bf16[1536,2,12]{2,1,0:T(2,128)(2,1)S(1)} reshape(bf16[4,2,4608]{2,1,0:T(2,128)(2,1)S(1)} %all-to-all-done.1) | data formatting | bytes 147456
  66.8 0.6 copy.52
  67.4 0.1 copy.44
  67.5 0.3 fusion.8
  67.8 0.1 convert_element_type.110
  67.9 10.9 %all-reduce.3 = bf16[8,768]{1,0:T(8,128)(2,1)S(1)} all-reduce(bf16[8,768]{1,0:T(8,128)(2,1)S(1)} %convert_element_type.110), channel_id=2, replica_groups=mesh['group'=2,'seq'=4,'fsdp'=4] {'fsdp'}, use_global_device_ids=true, to_apply=%region_3.0.clone | all-reduce | flops 6144 | bytes 24576
  78.9 9.4 %all-gather.8.cloned.1.call-done = bf16[768,1536]{1,0:T(8,128)(2,1)} async-done(((bf16[192,1536]{1,0:T(8,128)(2,1)}), bf16[768,1536]{1,0:T(8,128)(2,1)}) %all-gather.8.cloned.1.call-update) | async-done | bytes 2359312 | tf_op jit(solution)/shard_map/all_gather | solution.py:97
  88.3 3.2 %fusion.16 = bf16[1,2,768]{2,1,0:T(2,128)(2,1)S(1)} fusion(bf16[1536,768]{1,0:T(8,128)(2,1)} %all-gather.10.cloned.1.call-done, bf16[768,1536]{1,0:T(8,128)(2,1)} %all-gather.8.cloned.1.call-done, f32[2,1,1536]{2,1,0:T(1,128)S(1)} %slice_convert_fusion, pred[2]{0:T(512)(128)(4,1)S(1)} %fusion.56, bf16[8,768]{1,0:T(8,128)(2,1)S(1)} %all-reduce.3, ...), kind=kOutput, calls=%fused_computation.31 | convolution fusion | flops 9446400 | bytes 4737540 | tf_op jit(solution)/shard_map/dot_general | solution.py:137
  91.5 20.5 %all-gather.1 = bf16[16,2,768]{2,1,0:T(2,128)(2,1)S(1)} all-gather(bf16[1,2,768]{2,1,0:T(2,128)(2,1)S(1)} %fusion.16), channel_id=1, replica_groups=mesh['group'=2,'seq'=4,'fsdp'=4] {'seq','fsdp'}, dimensions={0}, use_global_device_ids=true | all-gather | bytes 52224 | tf_op jit(solution)/shard_map/all_gather | solution.py:151
  112.1 0.3 convert_reduce_fusion.1
  112.4 0.2 fusion.25
  112.6 0.2 convolution_convert_fusion.6
  112.7 0.1 reshape.336
  112.9 0.2 convolution_convert_fusion.5
  113.1 13.3 %all_gather.39 = bf16[32,192]{1,0:T(8,128)(2,1)S(1)} all-gather(bf16[8,192]{1,0:T(8,128)(2,1)S(1)} %convolution_convert_fusion.5), channel_id=1, replica_groups=mesh['group'=2,'seq'=4,'fsdp'=4] {'seq'}, dimensions={0}, use_global_device_ids=true | all-gather | bytes 15360 | tf_op jit(solution)/shard_map/all_gather | solution.py:171
  126.4 0.1 reshape.337
  126.5 0.2 convolution_convert_fusion.7
  126.6 13.3 %all_gather.36 = bf16[32,192]{1,0:T(8,128)(2,1)S(1)} all-gather(bf16[8,192]{1,0:T(8,128)(2,1)S(1)} %convolution_convert_fusion.7), channel_id=1, replica_groups=mesh['group'=2,'seq'=4,'fsdp'=4] {'seq'}, dimensions={0}, use_global_device_ids=true | all-gather | bytes 15360 | tf_op jit(solution)/shard_map/all_gather | solution.py:172
  139.9 0.1 reshape.335
  140.0 0.2 fusion.31
  140.2 0.1 fusion.23
  140.3 0.2 fusion.12
  140.6 0.1 convert_element_type.123
  140.6 0.2 convolution_convert_fusion.4
  140.8 0.8 copy.53
  141.7 17.2 %reduce-scatter.4.cloned.1.call-done = bf16[192,8]{1,0:T(8,128)(2,1)} async-done(((bf16[768,8]{1,0:T(8,128)(2,1)}), bf16[192,8]{1,0:T(8,128)(2,1)}) %reduce-scatter.4.cloned.1.call-update) | async-done | bytes 3088
  158.8 0.8 copy.54
  159.7 0.7 add_convert_fusion
  (54 shorter events, 0.4 us)
Async XLA Ops:
  6.5 134.1 %copy-start = (bf16[192,768]{1,0:T(8,128)(2,1)S(1)}, bf16[192,768]{1,0:T(8,128)(2,1)}, u32[]{:S(2)}) copy-start(bf16[192,768]{1,0:T(8,128)(2,1)} %param.25) | copy-start | bytes 884740
  6.5 2.2 %copy-start.1 = (bf16[2,256,1536]{2,1,0:T(8,128)(2,1)S(1)}, bf16[2,256,1536]{2,1,0:T(8,128)(2,1)}, u32[]{:S(2)}) copy-start(bf16[2,256,1536]{2,1,0:T(8,128)(2,1)} %param.14) | copy-start | bytes 4718596
  6.5 3.8 %copy-start.4 = (f32[1536]{0:T(1024)S(1)}, f32[1536]{0:T(1024)}, u32[]{:S(2)}) copy-start(f32[1536]{0:T(1024)} %param.15) | copy-start | bytes 18436
  6.5 29.9 %all-gather.6.cloned.1.call-start = ((), (), s32[]{:S(2)}) async-start(), calls=%async_computation.3 | async-start | bytes 2949120 | tf_op jit(solution)/shard_map/all_gather | solution.py:96
  7.3 71.7 %all-gather.10.cloned.1.call-start = ((), (), s32[]{:S(2)}) async-start(), calls=%async_computation.5 | async-start | bytes 2949120 | tf_op jit(solution)/shard_map/all_gather | solution.py:98
  8.0 80.3 %all-gather.8.cloned.1.call-start = ((), (), s32[]{:S(2)}) async-start(), calls=%async_computation.4 | async-start | bytes 2949120 | tf_op jit(solution)/shard_map/all_gather | solution.py:97
  9.1 1.8 %copy-start.12 = (u32[32]{0:T(128)S(1)}, u32[32]{0:T(128)}, u32[]{:S(2)}) copy-start(u32[32]{0:T(128)} %constant.98) | copy-start | bytes 388
  9.6 4.8 %copy-start.11 = (u32[32]{0:T(128)S(1)}, u32[32]{0:T(128)}, u32[]{:S(2)}) copy-start(u32[32]{0:T(128)} %constant.108) | copy-start | bytes 388
  9.6 5.4 %copy-start.9 = (s32[2]{0:T(128)S(1)}, s32[2]{0:T(128)}, u32[]{:S(2)}) copy-start(s32[2]{0:T(128)} %param.26) | copy-start | bytes 28
  36.4 7.4 %copy-start.2 = (bf16[384,768]{0,1:T(8,128)(2,1)S(1)}, bf16[384,768]{0,1:T(8,128)(2,1)}, u32[]{:S(2)}) copy-start(bf16[384,768]{0,1:T(8,128)(2,1)} %copy.37) | copy-start | bytes 1769476
  44.8 9.0 %all-to-all-start = ((bf16[8,12,384]{2,1,0:T(8,128)(2,1)}), bf16[8,12,384]{2,1,0:T(8,128)(2,1)S(1)}, u32[]{:S(2)}, u32[]{:S(2)}) async-start(bf16[8,12,384]{2,1,0:T(8,128)(2,1)} %copy.39), calls=%async_computation | async-start | bytes 196608 | tf_op jit(solution)/shard_map/all_to_all | solution.py:110
  53.9 7.1 %copy-start.3 = (bf16[384,768]{1,0:T(8,128)(2,1)S(1)}, bf16[384,768]{1,0:T(8,128)(2,1)}, u32[]{:S(2)}) copy-start(bf16[384,768]{1,0:T(8,128)(2,1)} %param.18) | copy-start | bytes 1769476
  54.4 6.8 %copy-start.10 = (u32[32]{0:T(128)S(1)}, u32[32]{0:T(128)}, u32[]{:S(2)}) copy-start(u32[32]{0:T(128)} %constant.116) | copy-start | bytes 388
  57.5 7.4 %all-to-all-start.1 = ((bf16[4,2,4608]{2,1,0:T(2,128)(2,1)}), bf16[4,2,4608]{2,1,0:T(2,128)(2,1)S(1)}, u32[]{:S(2)}, u32[]{:S(2)}) async-start(bf16[4,2,4608]{2,1,0:T(2,128)(2,1)} %reshape.362), calls=%async_computation.1 | async-start | bytes 147456 | tf_op jit(solution)/shard_map/all_to_all | solution.py:119
  60.8 98.0 %reduce-scatter.4.cloned.1.call-start = ((), (), s32[]{:S(2)}) async-start(), calls=%async_computation.6 | async-start | bytes 245760
  78.9 33.7 %copy-start.5 = (bf16[768,192]{0,1:T(8,128)(2,1)S(1)}, bf16[768,192]{0,1:T(8,128)(2,1)}, u32[]{:S(2)}) copy-start(bf16[768,192]{0,1:T(8,128)(2,1)} %param.22) | copy-start | bytes 884740
  78.9 33.7 %copy-start.8 = (f32[768]{0:T(1024)S(1)}, f32[768]{0:T(1024)}, u32[]{:S(2)}) copy-start(f32[768]{0:T(1024)} %param.21) | copy-start | bytes 9220
  78.9 34.0 %copy-start.6 = (bf16[768,192]{0,1:T(8,128)(2,1)S(1)}, bf16[768,192]{0,1:T(8,128)(2,1)}, u32[]{:S(2)}) copy-start(bf16[768,192]{0,1:T(8,128)(2,1)} %param.23) | copy-start | bytes 884740
  78.9 47.6 %copy-start.7 = (bf16[768,192]{0,1:T(8,128)(2,1)S(1)}, bf16[768,192]{0,1:T(8,128)(2,1)}, u32[]{:S(2)}) copy-start(bf16[768,192]{0,1:T(8,128)(2,1)} %param.24) | copy-start | bytes 884740
Sparse Core Ops, SparseCore 0:
  8.9 26.8 all-gather.5
  37.3 25.1 all-gather.9
  64.1 24.1 all-gather.7
  141.8 16.9 reduce-scatter.3
where the time goes:
time: 167 us
  blocking collectives  83.2 us (50%)
  waiting for transfers between devices  36.8 us (22%)
  between operations  16.1 us (10%)
  local copies, waits for them, and re-layouts  13 us (8%)
  matrix products  8.27 us (5%)
  starting transfers between devices  6.71 us (4%)
  other arithmetic  2.85 us (2%)
    unnamed x3, blocking collectives  30.9 us
    all_gather x1, blocking collectives, local(): lax.all_gather(embeds, ('seq', 'fsdp'), axis=0, tiled=True)  20.5 us
    unnamed x5, waiting for transfers between devices  19.3 us
    all_gather x1, blocking collectives, local(): lax.all_gather(key_local, 'seq', axis=0, tiled=True)  13.3 us
    all_gather x1, blocking collectives, local(): lax.all_gather(value_local, 'seq', axis=0, tiled=True)  13.3 us
    unnamed x41, local copies, waits for them, and re-layouts  10.4 us
    all_gather x1, waiting for transfers between devices, local(): lax.all_gather(w_out, 'fsdp', axis=0, tiled=True)  9.38 us
    all_to_all x1, waiting for transfers between devices, local(): lax.all_to_all(key_part.astype(jnp.bfloat16), 'fsdp', split_axis=0, conca...  5.61 us
  transfers between devices with their start and end apart: 6, of which 4 were waited for; matrix products, arithmetic and copies ran while one was open for 10% of the time, Pallas kernels for 0%

commit v1 on v0

--- a/solution.py
+++ b/solution.py
@@ -8,6 +8,17 @@
 HEADS = 16
 DILATION_STEP = 4
 EPSILON = 1e-06
+
+
+def gather_around(x, axis, dim):
+    ways = lax.axis_size(axis)
+    pieces = [x]
+    for far in range(1, ways):
+        pieces.append(
+            lax.ppermute(pieces[far - 1], axis, [(d, (d - 1) % ways) for d in range(ways)])
+        )
+    line = jnp.concatenate(pieces, axis=dim)
+    return jnp.roll(line, lax.axis_index(axis) * x.shape[dim], axis=dim)
 
 
 def layer_norm(inputs, norm_gain):
@@ -148,7 +159,7 @@
     targets = lax.axis_index("seq") * rows_dev + jnp.arange(rows_dev, dtype=jnp.int32)
     column_start = lax.axis_index("fsdp") * head_width
     all_embeds, all_order, all_present = (
-        lax.all_gather(embeds, ("seq", "fsdp"), axis=0, tiled=True),
+        gather_around(embeds, ("seq", "fsdp"), 0),
         lax.all_gather(seq_order, ("seq", "fsdp"), axis=0, tiled=True),
         lax.all_gather(present, ("seq", "fsdp"), axis=0, tiled=True),
     )

time: 167 us -> 239 us (1.43)
  starting transfers between devices: 6.71 us -> 64.9 us
  waiting for transfers between devices: 36.8 us -> 74.8 us
  blocking collectives: 83.2 us -> 57.2 us
    ppermute x0 -> x15, starting transfers between devices: none -> 58.2 us  [gather_around(): lax.ppermute(pieces[far - 1], axis, [(d, (d - 1) % ways) for d in range(w...]
    all_gather x1, waiting for transfers between devices: 0.02 us -> 23.4 us  [local(): lax.all_gather(w_query, 'fsdp', axis=0, tiled=True)]
    all_gather x1 -> x0, blocking collectives: 20.5 us -> none  [local(): lax.all_gather(embeds, ('seq', 'fsdp'), axis=0, tiled=True)]
    ppermute x0 -> x15, waiting for transfers between devices: none -> 15.6 us  [gather_around(): lax.ppermute(pieces[far - 1], axis, [(d, (d - 1) % ways) for d in range(w...]
    all_gather x1, waiting for transfers between devices: 9.38 us -> 0.02 us  [local(): lax.all_gather(w_out, 'fsdp', axis=0, tiled=True)]
    all_gather x1, waiting for transfers between devices: 0.02 us -> 9.01 us  [local(): lax.all_gather(w_proj, 'fsdp', axis=0, tiled=True)]
    unnamed x3, blocking collectives: 30.9 us -> 25.4 us
    unnamed x41 -> x38, local copies, waits for them, and re-layouts: 10.4 us -> 10.5 us
  transfers between devices with their start and end apart: 6 -> 21, of which waited for: 4 -> 17; matrix products, arithmetic and copies ran while one was open for 10% -> 7% of each run, Pallas kernels for 0% -> 0%
where the time goes in v1:
time: 239 us; the launch traced here: 238 us
  waiting for transfers between devices  74.8 us (31%)
  starting transfers between devices  64.9 us (27%)
  blocking collectives  57.2 us (24%)
  between operations  16 us (7%)
  local copies, waits for them, and re-layouts  13.4 us (6%)
  matrix products  9.3 us (4%)
  other arithmetic  2.84 us (1%)
    ppermute x15, starting transfers between devices, gather_around(): lax.ppermute(pieces[far - 1], axis, [(d, (d - 1) % ways) for d in range(w...  58.2 us
    unnamed x3, blocking collectives  25.4 us
    all_gather x1, waiting for transfers between devices, local(): lax.all_gather(w_query, 'fsdp', axis=0, tiled=True)  23.4 us
    unnamed x5, waiting for transfers between devices  19.3 us
    ppermute x15, waiting for transfers between devices, gather_around(): lax.ppermute(pieces[far - 1], axis, [(d, (d - 1) % ways) for d in range(w...  15.6 us
    all_gather x1, blocking collectives, local(): lax.all_gather(key_local, 'seq', axis=0, tiled=True)  13.3 us
    all_gather x1, blocking collectives, local(): lax.all_gather(value_local, 'seq', axis=0, tiled=True)  13.3 us
    unnamed x38, local copies, waits for them, and re-layouts  10.5 us
  transfers between devices with their start and end apart: 21, of which 17 were waited for; matrix products, arithmetic and copies ran while one was open for 7% of the time, Pallas kernels for 0%

profile of v1, /device:TPU:0, one launch (start us, length us, event | category | flops | bytes accessed | tf_op | source)
XLA Modules:
  0.0 238.4 jit_solution(1437240349066409731)
XLA Ops:
  6.5 0.7 all-gather.5.cloned.1.call-update
  7.3 0.7 all-gather.7.cloned.1.call-update
  8.1 0.7 all-gather.9.cloned.1.call-update
  9.0 0.5 fusion.2
  9.6 0.5 fusion.4
  10.2 2.1 copy.37
  12.3 23.4 %all-gather.5.cloned.1.call-done = bf16[1536,768]{1,0:T(8,128)(2,1)} async-done(((bf16[384,768]{1,0:T(8,128)(2,1)}), bf16[1536,768]{1,0:T(8,128)(2,1)}) %all-gather.5.cloned.1.call-update) | async-done | bytes 2359312 | tf_op jit(solution)/shard_map/all_gather | solution.py:107
  35.7 2.1 fusion.16
  37.8 5.2 %all-gather = bf16[4,2,768]{2,1,0:T(2,128)(2,1)S(1)} all-gather(bf16[1,2,768]{2,1,0:T(2,128)(2,1)S(1)} %fusion.16), channel_id=1, replica_groups=mesh['group'=2,'seq'=4,'fsdp'=4] {'fsdp'}, dimensions={0}, use_global_device_ids=true | all-gather | bytes 15360 | tf_op jit(solution)/shard_map/all_gather | solution.py:114
  43.0 1.3 fusion.6
  44.4 0.7 copy.39
  45.0 3.3 %all-to-all-start = ((bf16[8,12,384]{2,1,0:T(8,128)(2,1)}), bf16[8,12,384]{2,1,0:T(8,128)(2,1)S(1)}, u32[]{:S(2)}, u32[]{:S(2)}) async-start(bf16[8,12,384]{2,1,0:T(8,128)(2,1)} %copy.39), calls=%async_computation | async-start | bytes 196608 | tf_op jit(solution)/shard_map/all_to_all | solution.py:121
  49.0 5.0 %all-to-all-done = bf16[8,12,384]{2,1,0:T(8,128)(2,1)S(1)} async-done(((bf16[8,12,384]{2,1,0:T(8,128)(2,1)}), bf16[8,12,384]{2,1,0:T(8,128)(2,1)S(1)}, u32[]{:S(2)}, u32[]{:S(2)}) %all-to-all-start) | async-done | bytes 73760 | tf_op jit(solution)/shard_map/all_to_all | solution.py:121
  54.1 0.5 fusion.7
  54.7 0.4 convolution_convert_fusion
  55.0 0.6 copy.42
  55.7 2.1 reshape.360
  57.8 3.3 %all-to-all-start.1 = ((bf16[4,2,4608]{2,1,0:T(2,128)(2,1)}), bf16[4,2,4608]{2,1,0:T(2,128)(2,1)S(1)}, u32[]{:S(2)}, u32[]{:S(2)}) async-start(bf16[4,2,4608]{2,1,0:T(2,128)(2,1)} %reshape.360), calls=%async_computation.1 | async-start | bytes 147456 | tf_op jit(solution)/shard_map/all_to_all | solution.py:130
  61.2 0.3 copy.45
  61.5 0.6 dynamic-slice.3
  62.7 2.5 %all-to-all-done.1 = bf16[4,2,4608]{2,1,0:T(2,128)(2,1)S(1)} async-done(((bf16[4,2,4608]{2,1,0:T(2,128)(2,1)}), bf16[4,2,4608]{2,1,0:T(2,128)(2,1)S(1)}, u32[]{:S(2)}, u32[]{:S(2)}) %all-to-all-start.1) | async-done | bytes 73760 | tf_op jit(solution)/shard_map/all_to_all | solution.py:130
  65.2 1.8 reshape.361
  67.0 0.6 copy.52
  67.7 0.3 fusion.8
  68.2 10.9 %all-reduce.3 = bf16[8,768]{1,0:T(8,128)(2,1)S(1)} all-reduce(bf16[8,768]{1,0:T(8,128)(2,1)S(1)} %convert_element_type.110), channel_id=2, replica_groups=mesh['group'=2,'seq'=4,'fsdp'=4] {'fsdp'}, use_global_device_ids=true, to_apply=%region_3.0.clone | all-reduce | flops 6144 | bytes 24576
  79.2 9.0 %all-gather.9.cloned.1.call-done = bf16[1536,768]{1,0:T(8,128)(2,1)} async-done(((bf16[384,768]{1,0:T(8,128)(2,1)}), bf16[1536,768]{1,0:T(8,128)(2,1)}) %all-gather.9.cloned.1.call-update) | async-done | bytes 2359312 | tf_op jit(solution)/shard_map/all_gather | solution.py:109
  88.2 3.2 %fusion.15 = bf16[2,768]{1,0:T(2,128)(2,1)S(1)} fusion(bf16[1536,768]{1,0:T(8,128)(2,1)} %all-gather.9.cloned.1.call-done, bf16[768,1536]{1,0:T(8,128)(2,1)} %all-gather.7.cloned.1.call-done, f32[2,1,1536]{2,1,0:T(1,128)S(1)} %slice_convert_fusion, pred[2]{0:T(512)(128)(4,1)S(1)} %fusion.57, bf16[8,768]{1,0:T(8,128)(2,1)S(1)} %all-reduce.3, u32[]{:T(128)S(6)} %multiply.36), kind=kOutput, calls=%fused_computation.30 | convolution fusion | flops 9446400 | bytes 4737540 | tf_op jit(solution)/shard_map/dot_general | solution.py:148
  91.4 3.2 %collective-permute-start = (bf16[2,768]{1,0:T(2,128)(2,1)S(1)}, bf16[2,768]{1,0:T(2,128)(2,1)S(1)}, u32[]{:S(2)}, u32[]{:S(2)}) collective-permute-start(bf16[2,768]{1,0:T(2,128)(2,1)S(1)} %fusion.15), channel_id=1, source_target_pairs={{0,15},{1,0},{2,1},{3,2},{4,3},{5,4},{6,5},{7,6},{8,7},{9,8},{10,9... | collective-permute-start | bytes 9224 | tf_op jit(solution)/shard_map/ppermute | solution.py:18
  94.6 1.3 collective-permute-done
  95.9 4.4 %collective-permute-start.1 = (bf16[2,768]{1,0:T(2,128)(2,1)S(1)}, bf16[2,768]{1,0:T(2,128)(2,1)S(1)}, u32[]{:S(2)}, u32[]{:S(2)}) collective-permute-start(bf16[2,768]{1,0:T(2,128)(2,1)S(1)} %collective-permute-done), channel_id=1, source_target_pairs={{0,15},{1,0},{2,1},{3,2},{4,3},{5,4},{6,5},{7,6},{8,7},{9,8},{10,9... | collective-permute-start | bytes 9224 | tf_op jit(solution)/shard_map/ppermute | solution.py:18
  100.3 1.3 collective-permute-done.1
  101.6 4.4 %collective-permute-start.2 = (bf16[2,768]{1,0:T(2,128)(2,1)S(1)}, bf16[2,768]{1,0:T(2,128)(2,1)S(1)}, u32[]{:S(2)}, u32[]{:S(2)}) collective-permute-start(bf16[2,768]{1,0:T(2,128)(2,1)S(1)} %collective-permute-done.1), channel_id=1, source_target_pairs={{0,15},{1,0},{2,1},{3,2},{4,3},{5,4},{6,5},{7,6},{8,7},{9,8},{10,9... | collective-permute-start | bytes 9224 | tf_op jit(solution)/shard_map/ppermute | solution.py:18
  106.0 1.3 collective-permute-done.2
  107.3 4.4 %collective-permute-start.3 = (bf16[2,768]{1,0:T(2,128)(2,1)S(1)}, bf16[2,768]{1,0:T(2,128)(2,1)S(1)}, u32[]{:S(2)}, u32[]{:S(2)}) collective-permute-start(bf16[2,768]{1,0:T(2,128)(2,1)S(1)} %collective-permute-done.2), channel_id=1, source_target_pairs={{0,15},{1,0},{2,1},{3,2},{4,3},{5,4},{6,5},{7,6},{8,7},{9,8},{10,9... | collective-permute-start | bytes 9224 | tf_op jit(solution)/shard_map/ppermute | solution.py:18
  111.7 0.6 dynamic-slice
  113.1 4.4 %collective-permute-start.4 = (bf16[2,768]{1,0:T(2,128)(2,1)S(1)}, bf16[2,768]{1,0:T(2,128)(2,1)S(1)}, u32[]{:S(2)}, u32[]{:S(2)}) collective-permute-start(bf16[2,768]{1,0:T(2,128)(2,1)S(1)} %collective-permute-done.3), channel_id=1, source_target_pairs={{0,15},{1,0},{2,1},{3,2},{4,3},{5,4},{6,5},{7,6},{8,7},{9,8},{10,9... | collective-permute-start | bytes 9224 | tf_op jit(solution)/shard_map/ppermute | solution.py:18
  117.8 7.6 %all-reduce.4 = (s32[32]{0:T(128)S(1)}, s32[32]{0:T(128)S(1)}) all-reduce(s32[32]{0:T(128)S(1)} %dynamic-update-slice, s32[32]{0:T(128)S(1)} %fusion.56), channel_id=1, replica_groups=mesh['group'=2,'seq'=4,'fsdp'=4] {'seq','fsdp'}, use_global_device_ids=true, to_apply=%add | all-reduce | flops 64 | bytes 512
  125.4 1.9 collective-permute-start.5
  127.5 0.6 dynamic-slice.2
  129.0 6.8 %all-reduce.2 = s32[32]{0:T(128)S(1)} all-reduce(s32[32]{0:T(128)S(1)} %dynamic-update-slice.2), channel_id=1, replica_groups=mesh['group'=2,'seq'=4,'fsdp'=4] {'seq'}, use_global_device_ids=true, to_apply=%add.2 | all-reduce | flops 32 | bytes 256
  135.8 0.4 collective-permute-start.6
  136.1 1.3 collective-permute-done.6
  137.4 4.4 %collective-permute-start.7 = (bf16[2,768]{1,0:T(2,128)(2,1)S(1)}, bf16[2,768]{1,0:T(2,128)(2,1)S(1)}, u32[]{:S(2)}, u32[]{:S(2)}) collective-permute-start(bf16[2,768]{1,0:T(2,128)(2,1)S(1)} %collective-permute-done.6), channel_id=1, source_target_pairs={{0,15},{1,0},{2,1},{3,2},{4,3},{5,4},{6,5},{7,6},{8,7},{9,8},{10,9... | collective-permute-start | bytes 9224 | tf_op jit(solution)/shard_map/ppermute | solution.py:18
  141.9 1.3 collective-permute-done.7
  143.2 4.4 %collective-permute-start.8 = (bf16[2,768]{1,0:T(2,128)(2,1)S(1)}, bf16[2,768]{1,0:T(2,128)(2,1)S(1)}, u32[]{:S(2)}, u32[]{:S(2)}) collective-permute-start(bf16[2,768]{1,0:T(2,128)(2,1)S(1)} %collective-permute-done.7), channel_id=1, source_target_pairs={{0,15},{1,0},{2,1},{3,2},{4,3},{5,4},{6,5},{7,6},{8,7},{9,8},{10,9... | collective-permute-start | bytes 9224 | tf_op jit(solution)/shard_map/ppermute | solution.py:18
  147.6 1.3 collective-permute-done.8
  148.9 4.4 %collective-permute-start.9 = (bf16[2,768]{1,0:T(2,128)(2,1)S(1)}, bf16[2,768]{1,0:T(2,128)(2,1)S(1)}, u32[]{:S(2)}, u32[]{:S(2)}) collective-permute-start(bf16[2,768]{1,0:T(2,128)(2,1)S(1)} %collective-permute-done.8), channel_id=1, source_target_pairs={{0,15},{1,0},{2,1},{3,2},{4,3},{5,4},{6,5},{7,6},{8,7},{9,8},{10,9... | collective-permute-start | bytes 9224 | tf_op jit(solution)/shard_map/ppermute | solution.py:18
  153.4 1.2 collective-permute-done.9
  154.6 4.4 %collective-permute-start.10 = (bf16[2,768]{1,0:T(2,128)(2,1)S(1)}, bf16[2,768]{1,0:T(2,128)(2,1)S(1)}, u32[]{:S(2)}, u32[]{:S(2)}) collective-permute-start(bf16[2,768]{1,0:T(2,128)(2,1)S(1)} %collective-permute-done.9), channel_id=1, source_target_pairs={{0,15},{1,0},{2,1},{3,2},{4,3},{5,4},{6,5},{7,6},{8,7},{9,8},{10,9... | collective-permute-start | bytes 9224 | tf_op jit(solution)/shard_map/ppermute | solution.py:18
  159.0 1.3 collective-permute-done.10
  160.3 4.4 %collective-permute-start.11 = (bf16[2,768]{1,0:T(2,128)(2,1)S(1)}, bf16[2,768]{1,0:T(2,128)(2,1)S(1)}, u32[]{:S(2)}, u32[]{:S(2)}) collective-permute-start(bf16[2,768]{1,0:T(2,128)(2,1)S(1)} %collective-permute-done.10), channel_id=1, source_target_pairs={{0,15},{1,0},{2,1},{3,2},{4,3},{5,4},{6,5},{7,6},{8,7},{9,8},{10,9... | collective-permute-start | bytes 9224 | tf_op jit(solution)/shard_map/ppermute | solution.py:18
  164.7 1.3 collective-permute-done.11
  166.0 4.4 %collective-permute-start.12 = (bf16[2,768]{1,0:T(2,128)(2,1)S(1)}, bf16[2,768]{1,0:T(2,128)(2,1)S(1)}, u32[]{:S(2)}, u32[]{:S(2)}) collective-permute-start(bf16[2,768]{1,0:T(2,128)(2,1)S(1)} %collective-permute-done.11), channel_id=1, source_target_pairs={{0,15},{1,0},{2,1},{3,2},{4,3},{5,4},{6,5},{7,6},{8,7},{9,8},{10,9... | collective-permute-start | bytes 9224 | tf_op jit(solution)/shard_map/ppermute | solution.py:18
  170.5 1.2 collective-permute-done.12
  171.8 4.4 %collective-permute-start.13 = (bf16[2,768]{1,0:T(2,128)(2,1)S(1)}, bf16[2,768]{1,0:T(2,128)(2,1)S(1)}, u32[]{:S(2)}, u32[]{:S(2)}) collective-permute-start(bf16[2,768]{1,0:T(2,128)(2,1)S(1)} %collective-permute-done.12), channel_id=1, source_target_pairs={{0,15},{1,0},{2,1},{3,2},{4,3},{5,4},{6,5},{7,6},{8,7},{9,8},{10,9... | collective-permute-start | bytes 9224 | tf_op jit(solution)/shard_map/ppermute | solution.py:18
  176.2 1.3 collective-permute-done.13
  177.5 4.4 %collective-permute-start.14 = (bf16[2,768]{1,0:T(2,128)(2,1)S(1)}, bf16[2,768]{1,0:T(2,128)(2,1)S(1)}, u32[]{:S(2)}, u32[]{:S(2)}) collective-permute-start(bf16[2,768]{1,0:T(2,128)(2,1)S(1)} %collective-permute-done.13), channel_id=1, source_target_pairs={{0,15},{1,0},{2,1},{3,2},{4,3},{5,4},{6,5},{7,6},{8,7},{9,8},{10,9... | collective-permute-start | bytes 9224 | tf_op jit(solution)/shard_map/ppermute | solution.py:18
  182.0 1.2 collective-permute-done.14
  184.5 13.3 %all_gather.35 = bf16[32,192]{1,0:T(8,128)(2,1)S(1)} all-gather(bf16[8,192]{1,0:T(8,128)(2,1)S(1)} %convolution_convert_fusion.5), channel_id=1, replica_groups=mesh['group'=2,'seq'=4,'fsdp'=4] {'seq'}, dimensions={0}, use_global_device_ids=true | all-gather | bytes 15360 | tf_op jit(solution)/shard_map/all_gather | solution.py:182
  198.1 13.3 %all_gather.32 = bf16[32,192]{1,0:T(8,128)(2,1)S(1)} all-gather(bf16[8,192]{1,0:T(8,128)(2,1)S(1)} %convolution_convert_fusion.7), channel_id=1, replica_groups=mesh['group'=2,'seq'=4,'fsdp'=4] {'seq'}, dimensions={0}, use_global_device_ids=true | all-gather | bytes 15360 | tf_op jit(solution)/shard_map/all_gather | solution.py:183
  212.3 0.8 copy.53
  213.1 17.2 %reduce-scatter.4.cloned.1.call-done = bf16[192,8]{1,0:T(8,128)(2,1)} async-done(((bf16[768,8]{1,0:T(8,128)(2,1)}), bf16[192,8]{1,0:T(8,128)(2,1)}) %reduce-scatter.4.cloned.1.call-update) | async-done | bytes 3088
  230.3 0.8 copy.54
  231.1 0.7 add_convert_fusion
  (81 shorter events, 4.3 us)
Async XLA Ops:
  6.5 205.6 %copy-start = (bf16[192,768]{1,0:T(8,128)(2,1)S(1)}, bf16[192,768]{1,0:T(8,128)(2,1)}, u32[]{:S(2)}) copy-start(bf16[192,768]{1,0:T(8,128)(2,1)} %param.25) | copy-start | bytes 884740
  6.5 2.2 copy-start.1
  6.5 3.1 %copy-start.3 = (f32[1536]{0:T(1024)S(1)}, f32[1536]{0:T(1024)}, u32[]{:S(2)}) copy-start(f32[1536]{0:T(1024)} %param.15) | copy-start | bytes 18436
  6.5 29.2 %all-gather.5.cloned.1.call-start = ((), (), s32[]{:S(2)}) async-start(), calls=%async_computation.3 | async-start | bytes 2949120 | tf_op jit(solution)/shard_map/all_gather | solution.py:107
  7.3 71.9 %all-gather.7.cloned.1.call-start = ((), (), s32[]{:S(2)}) async-start(), calls=%async_computation.4 | async-start | bytes 2949120 | tf_op jit(solution)/shard_map/all_gather | solution.py:108
  8.0 80.2 %all-gather.9.cloned.1.call-start = ((), (), s32[]{:S(2)}) async-start(), calls=%async_computation.5 | async-start | bytes 2949120 | tf_op jit(solution)/shard_map/all_gather | solution.py:109
  45.0 9.0 %all-to-all-start = ((bf16[8,12,384]{2,1,0:T(8,128)(2,1)}), bf16[8,12,384]{2,1,0:T(8,128)(2,1)S(1)}, u32[]{:S(2)}, u32[]{:S(2)}) async-start(bf16[8,12,384]{2,1,0:T(8,128)(2,1)} %copy.39), calls=%async_computation | async-start | bytes 196608 | tf_op jit(solution)/shard_map/all_to_all | solution.py:121
  54.1 7.1 %copy-start.2 = (bf16[384,768]{1,0:T(8,128)(2,1)S(1)}, bf16[384,768]{1,0:T(8,128)(2,1)}, u32[]{:S(2)}) copy-start(bf16[384,768]{1,0:T(8,128)(2,1)} %param.18) | copy-start | bytes 1769476
  54.6 6.8 %copy-start.11 = (u32[32]{0:T(128)S(1)}, u32[32]{0:T(128)}, u32[]{:S(2)}) copy-start(u32[32]{0:T(128)} %constant.139) | copy-start | bytes 388
  57.8 7.4 %all-to-all-start.1 = ((bf16[4,2,4608]{2,1,0:T(2,128)(2,1)}), bf16[4,2,4608]{2,1,0:T(2,128)(2,1)S(1)}, u32[]{:S(2)}, u32[]{:S(2)}) async-start(bf16[4,2,4608]{2,1,0:T(2,128)(2,1)} %reshape.360), calls=%async_computation.1 | async-start | bytes 147456 | tf_op jit(solution)/shard_map/all_to_all | solution.py:130
  61.1 169.2 %reduce-scatter.4.cloned.1.call-start = ((), (), s32[]{:S(2)}) async-start(), calls=%async_computation.6 | async-start | bytes 245760
  79.1 32.6 %copy-start.10 = (u32[32]{0:T(128)S(1)}, u32[32]{0:T(128)}, u32[]{:S(2)}) copy-start(u32[32]{0:T(128)} %constant.121) | copy-start | bytes 388
  79.1 38.4 %copy-start.8 = (s32[2]{0:T(128)S(1)}, s32[2]{0:T(128)}, u32[]{:S(2)}) copy-start(s32[2]{0:T(128)} %param.26) | copy-start | bytes 28
  79.1 48.4 %copy-start.9 = (u32[32]{0:T(128)S(1)}, u32[32]{0:T(128)}, u32[]{:S(2)}) copy-start(u32[32]{0:T(128)} %constant.131) | copy-start | bytes 388
  79.1 104.9 %copy-start.4 = (bf16[768,192]{0,1:T(8,128)(2,1)S(1)}, bf16[768,192]{0,1:T(8,128)(2,1)}, u32[]{:S(2)}) copy-start(bf16[768,192]{0,1:T(8,128)(2,1)} %param.22) | copy-start | bytes 884740
  79.1 104.9 %copy-start.7 = (f32[768]{0:T(1024)S(1)}, f32[768]{0:T(1024)}, u32[]{:S(2)}) copy-start(f32[768]{0:T(1024)} %param.21) | copy-start | bytes 9220
  79.1 105.1 %copy-start.5 = (bf16[768,192]{0,1:T(8,128)(2,1)S(1)}, bf16[768,192]{0,1:T(8,128)(2,1)}, u32[]{:S(2)}) copy-start(bf16[768,192]{0,1:T(8,128)(2,1)} %param.23) | copy-start | bytes 884740
  79.2 118.8 %copy-start.6 = (bf16[768,192]{0,1:T(8,128)(2,1)S(1)}, bf16[768,192]{0,1:T(8,128)(2,1)}, u32[]{:S(2)}) copy-start(bf16[768,192]{0,1:T(8,128)(2,1)} %param.24) | copy-start | bytes 884740
  91.4 4.5 %collective-permute-start = (bf16[2,768]{1,0:T(2,128)(2,1)S(1)}, bf16[2,768]{1,0:T(2,128)(2,1)S(1)}, u32[]{:S(2)}, u32[]{:S(2)}) collective-permute-start(bf16[2,768]{1,0:T(2,128)(2,1)S(1)} %fusion.15), channel_id=1, source_target_pairs={{0,15},{1,0},{2,1},{3,2},{4,3},{5,4},{6,5},{7,6},{8,7},{9,8},{10,9... | collective-permute-start | bytes 9224 | tf_op jit(solution)/shard_map/ppermute | solution.py:18
  95.9 5.7 %collective-permute-start.1 = (bf16[2,768]{1,0:T(2,128)(2,1)S(1)}, bf16[2,768]{1,0:T(2,128)(2,1)S(1)}, u32[]{:S(2)}, u32[]{:S(2)}) collective-permute-start(bf16[2,768]{1,0:T(2,128)(2,1)S(1)} %collective-permute-done), channel_id=1, source_target_pairs={{0,15},{1,0},{2,1},{3,2},{4,3},{5,4},{6,5},{7,6},{8,7},{9,8},{10,9... | collective-permute-start | bytes 9224 | tf_op jit(solution)/shard_map/ppermute | solution.py:18
  101.6 5.7 %collective-permute-start.2 = (bf16[2,768]{1,0:T(2,128)(2,1)S(1)}, bf16[2,768]{1,0:T(2,128)(2,1)S(1)}, u32[]{:S(2)}, u32[]{:S(2)}) collective-permute-start(bf16[2,768]{1,0:T(2,128)(2,1)S(1)} %collective-permute-done.1), channel_id=1, source_target_pairs={{0,15},{1,0},{2,1},{3,2},{4,3},{5,4},{6,5},{7,6},{8,7},{9,8},{10,9... | collective-permute-start | bytes 9224 | tf_op jit(solution)/shard_map/ppermute | solution.py:18
  107.3 5.7 %collective-permute-start.3 = (bf16[2,768]{1,0:T(2,128)(2,1)S(1)}, bf16[2,768]{1,0:T(2,128)(2,1)S(1)}, u32[]{:S(2)}, u32[]{:S(2)}) collective-permute-start(bf16[2,768]{1,0:T(2,128)(2,1)S(1)} %collective-permute-done.2), channel_id=1, source_target_pairs={{0,15},{1,0},{2,1},{3,2},{4,3},{5,4},{6,5},{7,6},{8,7},{9,8},{10,9... | collective-permute-start | bytes 9224 | tf_op jit(solution)/shard_map/ppermute | solution.py:18
  113.1 12.4 %collective-permute-start.4 = (bf16[2,768]{1,0:T(2,128)(2,1)S(1)}, bf16[2,768]{1,0:T(2,128)(2,1)S(1)}, u32[]{:S(2)}, u32[]{:S(2)}) collective-permute-start(bf16[2,768]{1,0:T(2,128)(2,1)S(1)} %collective-permute-done.3), channel_id=1, source_target_pairs={{0,15},{1,0},{2,1},{3,2},{4,3},{5,4},{6,5},{7,6},{8,7},{9,8},{10,9... | collective-permute-start | bytes 9224 | tf_op jit(solution)/shard_map/ppermute | solution.py:18
  125.4 10.3 %collective-permute-start.5 = (bf16[2,768]{1,0:T(2,128)(2,1)S(1)}, bf16[2,768]{1,0:T(2,128)(2,1)S(1)}, u32[]{:S(2)}, u32[]{:S(2)}) collective-permute-start(bf16[2,768]{1,0:T(2,128)(2,1)S(1)} %collective-permute-done.4), channel_id=1, source_target_pairs={{0,15},{1,0},{2,1},{3,2},{4,3},{5,4},{6,5},{7,6},{8,7},{9,8},{10,9... | collective-permute-start | bytes 9224 | tf_op jit(solution)/shard_map/ppermute | solution.py:18
  135.8 1.7 collective-permute-start.6
  137.4 5.7 %collective-permute-start.7 = (bf16[2,768]{1,0:T(2,128)(2,1)S(1)}, bf16[2,768]{1,0:T(2,128)(2,1)S(1)}, u32[]{:S(2)}, u32[]{:S(2)}) collective-permute-start(bf16[2,768]{1,0:T(2,128)(2,1)S(1)} %collective-permute-done.6), channel_id=1, source_target_pairs={{0,15},{1,0},{2,1},{3,2},{4,3},{5,4},{6,5},{7,6},{8,7},{9,8},{10,9... | collective-permute-start | bytes 9224 | tf_op jit(solution)/shard_map/ppermute | solution.py:18
  143.2 5.7 %collective-permute-start.8 = (bf16[2,768]{1,0:T(2,128)(2,1)S(1)}, bf16[2,768]{1,0:T(2,128)(2,1)S(1)}, u32[]{:S(2)}, u32[]{:S(2)}) collective-permute-start(bf16[2,768]{1,0:T(2,128)(2,1)S(1)} %collective-permute-done.7), channel_id=1, source_target_pairs={{0,15},{1,0},{2,1},{3,2},{4,3},{5,4},{6,5},{7,6},{8,7},{9,8},{10,9... | collective-permute-start | bytes 9224 | tf_op jit(solution)/shard_map/ppermute | solution.py:18
  148.9 5.7 %collective-permute-start.9 = (bf16[2,768]{1,0:T(2,128)(2,1)S(1)}, bf16[2,768]{1,0:T(2,128)(2,1)S(1)}, u32[]{:S(2)}, u32[]{:S(2)}) collective-permute-start(bf16[2,768]{1,0:T(2,128)(2,1)S(1)} %collective-permute-done.8), channel_id=1, source_target_pairs={{0,15},{1,0},{2,1},{3,2},{4,3},{5,4},{6,5},{7,6},{8,7},{9,8},{10,9... | collective-permute-start | bytes 9224 | tf_op jit(solution)/shard_map/ppermute | solution.py:18
  154.6 5.7 %collective-permute-start.10 = (bf16[2,768]{1,0:T(2,128)(2,1)S(1)}, bf16[2,768]{1,0:T(2,128)(2,1)S(1)}, u32[]{:S(2)}, u32[]{:S(2)}) collective-permute-start(bf16[2,768]{1,0:T(2,128)(2,1)S(1)} %collective-permute-done.9), channel_id=1, source_target_pairs={{0,15},{1,0},{2,1},{3,2},{4,3},{5,4},{6,5},{7,6},{8,7},{9,8},{10,9... | collective-permute-start | bytes 9224 | tf_op jit(solution)/shard_map/ppermute | solution.py:18
  160.3 5.7 %collective-permute-start.11 = (bf16[2,768]{1,0:T(2,128)(2,1)S(1)}, bf16[2,768]{1,0:T(2,128)(2,1)S(1)}, u32[]{:S(2)}, u32[]{:S(2)}) collective-permute-start(bf16[2,768]{1,0:T(2,128)(2,1)S(1)} %collective-permute-done.10), channel_id=1, source_target_pairs={{0,15},{1,0},{2,1},{3,2},{4,3},{5,4},{6,5},{7,6},{8,7},{9,8},{10,9... | collective-permute-start | bytes 9224 | tf_op jit(solution)/shard_map/ppermute | solution.py:18
  166.0 5.7 %collective-permute-start.12 = (bf16[2,768]{1,0:T(2,128)(2,1)S(1)}, bf16[2,768]{1,0:T(2,128)(2,1)S(1)}, u32[]{:S(2)}, u32[]{:S(2)}) collective-permute-start(bf16[2,768]{1,0:T(2,128)(2,1)S(1)} %collective-permute-done.11), channel_id=1, source_target_pairs={{0,15},{1,0},{2,1},{3,2},{4,3},{5,4},{6,5},{7,6},{8,7},{9,8},{10,9... | collective-permute-start | bytes 9224 | tf_op jit(solution)/shard_map/ppermute | solution.py:18
  171.8 5.7 %collective-permute-start.13 = (bf16[2,768]{1,0:T(2,128)(2,1)S(1)}, bf16[2,768]{1,0:T(2,128)(2,1)S(1)}, u32[]{:S(2)}, u32[]{:S(2)}) collective-permute-start(bf16[2,768]{1,0:T(2,128)(2,1)S(1)} %collective-permute-done.12), channel_id=1, source_target_pairs={{0,15},{1,0},{2,1},{3,2},{4,3},{5,4},{6,5},{7,6},{8,7},{9,8},{10,9... | collective-permute-start | bytes 9224 | tf_op jit(solution)/shard_map/ppermute | solution.py:18
  177.5 5.7 %collective-permute-start.14 = (bf16[2,768]{1,0:T(2,128)(2,1)S(1)}, bf16[2,768]{1,0:T(2,128)(2,1)S(1)}, u32[]{:S(2)}, u32[]{:S(2)}) collective-permute-start(bf16[2,768]{1,0:T(2,128)(2,1)S(1)} %collective-permute-done.13), channel_id=1, source_target_pairs={{0,15},{1,0},{2,1},{3,2},{4,3},{5,4},{6,5},{7,6},{8,7},{9,8},{10,9... | collective-permute-start | bytes 9224 | tf_op jit(solution)/shard_map/ppermute | solution.py:18
Sparse Core Ops, SparseCore 0:
  8.9 26.7 all-gather.4
  37.3 25.0 all-gather.6
  64.0 24.2 all-gather.8
  213.2 16.9 reduce-scatter.3
